TPU v7x, 128 devices: a whole 4x4x4 slice. The times are simulated.
128 devices in a mesh: dp: 4 (over y_lo, core), ctx: 32 (over z, x, y_hi).
Axes of the slice: x: 4, y: 4 (y_hi: 2, y_lo: 2; y = y_hi * 2 + y_lo), z: 4, core: 2. Of those that a mesh axis runs over, the one named last changes fastest.
Arguments:
- queries: bfloat16 [4, 32768, 1024], P('dp', 'ctx'), may hold values from -160 to 160
- keys: bfloat16 [4, 32768, 1024], P('dp', 'ctx'), may hold values from -14 to 14
- values: bfloat16 [4, 32768, 1024], P('dp', 'ctx'), may hold values from -4.5 to 4.5
- cotangent: bfloat16 [4, 32768, 1024], P('dp', 'ctx'), may hold values from -6 to 6
- gain: float32 [1024], replicated, may hold values from 0.1 to 1.9
Outputs:
- attended: bfloat16 [4, 32768, 1024], P('dp', 'ctx')
- grad_queries: bfloat16 [4, 32768, 1024], P('dp', 'ctx')
- grad_keys: bfloat16 [4, 32768, 1024], P('dp', 'ctx')
- grad_values: bfloat16 [4, 32768, 1024], P('dp', 'ctx')
- gain_grad: float32 [1024], replicated
All inputs are finite; a program needn't handle non-finite values.
Results may differ from a plain program's by a relative error of at most 0.019.
The roundings to bfloat16 on the way count: a program that leaves them out, or rounds other values in their place, can miss the bound.
Values may be sent and summed in bfloat16 or wider, within the bound.
A program may use at most 192 MiB of HBM per device.

v0:
```python
import jax
import jax.numpy as jnp
from jax import lax
from jax.sharding import PartitionSpec as P

H = 8
HD = 128
BLOCK = 128
STRIDE = 1024
SUMMARY = 8
NEG = -1e30


def from_behind(value, axis, steps):
    count = lax.axis_size(axis)
    first, last = (max(0, -steps), min(count, count - steps))
    return lax.ppermute(value, axis, [(source, source + steps) for source in range(first, last)])


def to_rows(block_array):
    batch, blocks, heads, width = block_array.shape
    return block_array.transpose(0, 2, 1, 3).reshape(batch, heads, blocks * width)


def to_blocks(row_array, blocks):
    batch, heads, length = row_array.shape
    return row_array.reshape(batch, heads, blocks, length // blocks).transpose(0, 2, 1, 3)


def per_device(queries, keys, values, cotangent, gain):
    f32 = jnp.float32
    bf16 = jnp.bfloat16
    batch, length, width = queries.shape
    blocks = length // BLOCK
    segs = length // STRIDE
    own_sums = segs * SUMMARY
    ctx_count = lax.axis_size("ctx")
    rank = lax.axis_index("ctx")
    scale = HD ** (-0.5)
    scaled = (queries.astype(f32) * gain).astype(bf16)
    rim_keys, rim_values = from_behind(
        (keys[:, length - BLOCK :], values[:, length - BLOCK :]), "ctx", 1
    )
    own_sum_keys = keys.reshape(batch, segs, STRIDE, width)[:, :, STRIDE - SUMMARY :].reshape(
        batch, own_sums, width
    )
    own_sum_values = values.reshape(batch, segs, STRIDE, width)[:, :, STRIDE - SUMMARY :].reshape(
        batch, own_sums, width
    )
    sum_keys, sum_values = (
        lax.all_gather(own_sum_keys, "ctx", axis=1, tiled=True),
        lax.all_gather(own_sum_values, "ctx", axis=1, tiled=True),
    )
    total_sums = sum_keys.shape[1]
    sum_keys = sum_keys.reshape(batch, total_sums, H, HD)
    sum_values = sum_values.reshape(batch, total_sums, H, HD)
    ext_keys = jnp.concatenate([rim_keys, keys], 1).reshape(batch, blocks + 1, BLOCK, H, HD)
    ext_values = jnp.concatenate([rim_values, values], 1).reshape(batch, blocks + 1, BLOCK, H, HD)
    band_keys = jnp.concatenate([ext_keys[:, :-1], ext_keys[:, 1:]], 2)
    band_values = jnp.concatenate([ext_values[:, :-1], ext_values[:, 1:]], 2)
    query_blocks = scaled.reshape(batch, blocks, BLOCK, H, HD)
    scaled_rows = scaled.reshape(batch, length, H, HD)
    grad_rows = cotangent.reshape(batch, length, H, HD)
    grad_blocks = cotangent.reshape(batch, blocks, BLOCK, H, HD)
    query_index = jnp.arange(BLOCK, dtype=jnp.int32)[:, None]
    key_index = jnp.arange(2 * BLOCK, dtype=jnp.int32)[None, :]
    band = (key_index > query_index) & (key_index <= query_index + BLOCK)
    global_block = rank * blocks + jnp.arange(blocks, dtype=jnp.int32)
    band_mask = band[None] & ((global_block > 0)[:, None, None] | (key_index >= BLOCK)[None])
    band_mask = band_mask[None, :, None]
    slot = jnp.arange(total_sums, dtype=jnp.int32)
    sum_pos = slot // SUMMARY * STRIDE + STRIDE - SUMMARY + slot % SUMMARY
    query_pos = rank * length + jnp.arange(length, dtype=jnp.int32)
    sum_mask = (query_pos[:, None] - sum_pos[None, :] >= BLOCK)[None, None]
    band_scores = (
        jnp.einsum("bnqhd,bnkhd->bnhqk", query_blocks, band_keys, preferred_element_type=f32)
        * scale
    )
    band_scores = jnp.where(band_mask, band_scores, NEG)
    sum_scores = (
        jnp.einsum("bqhd,bshd->bhqs", scaled_rows, sum_keys, preferred_element_type=f32) * scale
    )
    sum_scores = jnp.where(sum_mask, sum_scores, NEG)
    top = jnp.maximum(to_rows(jnp.max(band_scores, -1)), jnp.max(sum_scores, -1))
    band_exp = jnp.where(band_mask, jnp.exp(band_scores - to_blocks(top, blocks)[..., None]), 0.0)
    sum_exp = jnp.where(sum_mask, jnp.exp(sum_scores - top[..., None]), 0.0)
    total = to_rows(jnp.sum(band_exp, -1)) + jnp.sum(sum_exp, -1)
    band_prob = band_exp / to_blocks(total, blocks)[..., None]
    sum_prob = sum_exp / total[..., None]
    band_prob_b = band_prob.astype(bf16)
    sum_prob_b = sum_prob.astype(bf16)
    mixed = jnp.einsum(
        "bnhqk,bnkhd->bnqhd", band_prob_b, band_values, preferred_element_type=f32
    ).reshape(batch, length, H, HD)
    mixed = mixed + jnp.einsum(
        "bhqs,bshd->bqhd", sum_prob_b, sum_values, preferred_element_type=f32
    )
    attended = mixed.reshape(batch, length, width).astype(bf16)
    delta = jnp.sum(
        grad_rows.astype(f32) * attended.reshape(batch, length, H, HD).astype(f32), -1
    ).transpose(0, 2, 1)
    band_dprob = jnp.einsum(
        "bnqhd,bnkhd->bnhqk", grad_blocks, band_values, preferred_element_type=f32
    )
    sum_dprob = jnp.einsum("bqhd,bshd->bhqs", grad_rows, sum_values, preferred_element_type=f32)
    band_ds = (band_prob * (band_dprob - to_blocks(delta, blocks)[..., None]) * scale).astype(bf16)
    sum_ds = (sum_prob * (sum_dprob - delta[..., None]) * scale).astype(bf16)
    band_dv = jnp.einsum("bnhqk,bnqhd->bnkhd", band_prob_b, grad_blocks, preferred_element_type=f32)
    band_dk = jnp.einsum("bnhqk,bnqhd->bnkhd", band_ds, query_blocks, preferred_element_type=f32)
    rim_dk, rim_dv = from_behind((band_dk[:, 0, :BLOCK], band_dv[:, 0, :BLOCK]), "ctx", -1)
    sum_dv = jnp.einsum(
        "bhqs,bqhd->bshd", sum_prob_b, grad_rows, preferred_element_type=f32
    ).reshape(batch, total_sums, width)
    sum_dk = jnp.einsum("bhqs,bqhd->bshd", sum_ds, scaled_rows, preferred_element_type=f32).reshape(
        batch, total_sums, width
    )
    whole_dk, whole_dv = lax.psum((sum_dk, sum_dv), "ctx")
    owned_dk = lax.dynamic_slice_in_dim(whole_dk, rank * own_sums, own_sums, 1)
    owned_dv = lax.dynamic_slice_in_dim(whole_dv, rank * own_sums, own_sums, 1)

    def fold_band(pairs, received, owned):
        later = jnp.concatenate([pairs[:, 1:, :BLOCK], received[:, None]], 1)
        folded = (pairs[:, :, BLOCK:] + later).reshape(batch, segs, STRIDE, width)
        folded = folded.at[:, :, STRIDE - SUMMARY :].add(owned.reshape(batch, segs, SUMMARY, width))
        return folded.reshape(batch, length, width).astype(bf16)

    grad_values = fold_band(band_dv, rim_dv, owned_dv)
    grad_keys = fold_band(band_dk, rim_dk, owned_dk)
    grad_scaled = jnp.einsum(
        "bnhqk,bnkhd->bnqhd", band_ds, band_keys, preferred_element_type=f32
    ).reshape(batch, length, H, HD)
    grad_scaled = grad_scaled + jnp.einsum(
        "bhqs,bshd->bqhd", sum_ds, sum_keys, preferred_element_type=f32
    )
    grad_scaled = grad_scaled.reshape(batch, length, width)
    grad_queries = (grad_scaled * gain).astype(bf16)
    gain_part = jnp.sum(grad_scaled * queries.astype(f32), (0, 1))
    gain_total = lax.psum(gain_part, ("dp", "ctx"))
    token_count = batch * lax.axis_size("dp") * length * ctx_count
    gain_grad = gain_total * token_count ** (-0.5)
    return (attended, grad_queries, grad_keys, grad_values, gain_grad)


def solution(mesh):
    in_specs = (
        P("dp", "ctx", None),
        P("dp", "ctx", None),
        P("dp", "ctx", None),
        P("dp", "ctx", None),
        P(),
    )
    out_specs = (
        P("dp", "ctx", None),
        P("dp", "ctx", None),
        P("dp", "ctx", None),
        P("dp", "ctx", None),
        P(),
    )
    return jax.shard_map(
        per_device, mesh=mesh, in_specs=in_specs, out_specs=out_specs, check_vma=False
    )
```

profile of v0, /device:TPU:8, one launch (start us, length us, event | category | flops | bytes accessed | tf_op | source)
XLA Modules:
  0.0 754.5 jit_solution(17129775396608550831)
XLA Ops:
  9.0 4.2 collective-permute-start
  14.9 4.8 collective-permute-start.1
  26.7 93.4 %all-gather = bf16[1,1,256,1024]{3,2,1,0:T(8,128)(2,1)S(1)} all-gather(bf16[1,1,8,1024]{3,2,1,0:T(8,128)(2,1)S(1)} %slice.118), channel_id=2, replica_groups=mesh['dp'=4,'ctx'=32] {'ctx'}, dimensions={2}, use_global_device_ids=true | all-gather | bytes 540672 | tf_op jit(solution)/shard_map/all_gather | solution.py:51
  120.3 95.3 %all-gather.1 = bf16[1,1,256,1024]{3,2,1,0:T(8,128)(2,1)} all-gather(bf16[1,1,8,1024]{3,2,1,0:T(8,128)(2,1)S(1)} %slice.121), channel_id=3, replica_groups=mesh['dp'=4,'ctx'=32] {'ctx'}, dimensions={2}, use_global_device_ids=true | all-gather | bytes 540672 | tf_op jit(solution)/shard_map/all_gather | solution.py:52
  219.8 6.6 fusion.3
  230.4 4.1 copy.86
  251.7 5.2 fusion.2
  256.9 5.7 fusion.5
  274.6 4.3 copy.81
  279.0 5.4 copy.84
  284.4 9.3 %convolution_bitcast_fusion = f32[1,8,256,8,128]{4,2,3,1,0:T(8,128)} fusion(bf16[8,128,8,128]{3,2,1,0:T(8,128)(2,1)} %bitcast.200, f32[8,8,128,256]{3,2,1,0:T(8,128)} %get-tuple-element.53, f32[8,8,128]{2,1,0:T(8,128)S(1)} %fusion.28, f32[8,8,128]{2,1,0:T(8,128)S(1)} %fusion.29, pred[8,128,256]{2,1,0:T(8,128)(4,1)S(1)} %broadcast_and_fusion), kind=kOutput, calls=%fused_computation.27 | convolution fusion | flops 549453824 | bytes 19202048 | tf_op jit(solution)/shard_map/bnhqk,bnqhd->bnkhd/dot_general | solution.py:108
  293.8 6.1 fusion.16
  300.0 7.2 multiply_reduce_fusion
  307.1 17.9 %fusion.1 = bf16[8,8,128,256]{3,2,1,0:T(8,128)(2,1)S(1)} fusion(f32[8,8,128]{2,1,0:T(8,128)} %bitcast.208, bf16[1,8,128,8,128]{4,2,3,1,0:T(8,128)(2,1)} %copy-done.17, bf16[1,8,128,8,128]{4,2,3,1,0:T(8,128)(2,1)} %copy-done.16, bf16[8,128,8,128]{3,2,1,0:T(8,128)(2,1)} %bitcast.201, f32[8,8,128]{2,1,0:T(8,128)} %copy-done.25, f32[8,8,128]{2,1,0:T(8,128)} %copy-done.21, ...), kind=kOutput, calls=%fused_computation.2 | convolution fusion | flops 564133888 | bytes 19234816 | tf_op jit(solution)/shard_map/bnqhd,bnkhd->bnhqk/dot_general | solution.py:102
  325.1 4.4 fusion.14
  329.5 4.4 copy.88
  333.9 5.5 copy.93
  339.4 8.1 %multiply_convert_fusion = bf16[8,1024,256]{1,2,0:T(8,128)(2,1)S(1)} fusion(f32[8,1024]{1,0:T(8,128)S(1)} %bitcast.209, bf16[1024,8,128]{0,2,1:T(8,128)(2,1)} %bitcast.198, bf16[256,8,128]{0,2,1:T(8,128)(2,1)} %bitcast.206, f32[8,1024]{1,0:T(8,128)S(1)} %copy-done.24, f32[8,1024]{1,0:T(8,128)S(1)} %copy-done.20, f32[8,1024,256]{1,2,0:T(8,128)} %get-tuple-element.55, ...), kind=kOutput, calls=%fused_computation.3 | convolution fusion | flops 555745280 | bytes 15564800 | tf_op jit(solution)/shard_map/bqhd,bshd->bhqs/dot_general | solution.py:105
  353.0 5.4 copy.94
  361.7 4.2 convolution_bitcast_fusion.1
  373.4 68.5 %psum.23 = f32[1024]{0:T(1024)S(1)} all-reduce(f32[1024]{0:T(1024)S(1)} %get-tuple-element.46), channel_id=1, replica_groups=mesh['dp'=4,'ctx'=32] {'dp','ctx'}, use_global_device_ids=true, to_apply=%region_8.9 | all-reduce | flops 1024 | bytes 8192 | tf_op jit(solution)/shard_map/psum | solution.py:138
  442.5 4.3 slice.123
  446.8 4.5 slice.127
  453.8 6.3 slice_add_fusion.1
  460.1 5.6 copy.96
  469.8 4.4 copy.103
  474.2 7.2 copy.138
  483.3 238.8 %all-reduce.3.cloned.1.call-done = (f32[1,256,1024]{1,2,0:T(8,128)}, f32[1,256,1024]{1,2,0:T(8,128)}) async-done(((f32[1,256,1024]{1,2,0:T(8,128)}, f32[1,256,1024]{1,2,0:T(8,128)}), (f32[1,256,1024]{1,2,0:T(8,128)}, f32[1,256,1024]{1,2,0:T(8,128)})) %all-reduce.3.cloned.1.call-update) | async-done | bytes 2097168 | tf_op jit(solution)/shard_map/psum | solution.py:117
  725.4 7.1 convert_element_type.88
  732.5 4.5 copy.111
  737.8 5.1 convert_element_type.87
  742.9 4.3 copy.110
  (134 shorter events, 77.4 us)
Async XLA Ops:
  7.2 16.1 %copy-start.22 = (f32[1024]{0:T(1024)S(1)}, f32[1024]{0:T(1024)}, u32[]{:S(2)}) copy-start(f32[1024]{0:T(1024)} %param.13) | copy-start | bytes 12292
  7.2 16.1 %copy-start.2 = (bf16[1,1024,1024]{2,1,0:T(8,128)(2,1)S(1)}, bf16[1,1024,1024]{2,1,0:T(8,128)(2,1)}, u32[]{:S(2)}) copy-start(bf16[1,1024,1024]{2,1,0:T(8,128)(2,1)} %param.9) | copy-start | bytes 6291460
  7.2 714.9 %all-reduce.3.cloned.1.call-start = ((), (), s32[]{:S(2)}) async-start(), calls=%async_computation | async-start | bytes 4194304 | tf_op jit(solution)/shard_map/psum | solution.py:117
  9.0 256.1 %collective-permute-start = (bf16[1,128,1024]{2,1,0:T(8,128)(2,1)}, bf16[1,128,1024]{2,1,0:T(8,128)(2,1)S(1)}, u32[]{:S(2)}, u32[]{:S(2)}) collective-permute-start(bf16[1,128,1024]{2,1,0:T(8,128)(2,1)} %slice.100), channel_id=1, source_target_pairs={{0,1},{1,2},{2,3},{3,4},{4,5},{5,6},{6,7},{7,8},{8,9},{9,10},{10,1... | collective-permute-start | bytes 786440 | tf_op jit(solution)/shard_map/ppermute | solution.py:17
  14.9 231.6 %collective-permute-start.1 = (bf16[1,128,1024]{2,1,0:T(8,128)(2,1)}, bf16[1,128,1024]{2,1,0:T(8,128)(2,1)}, u32[]{:S(2)}, u32[]{:S(2)}) collective-permute-start(bf16[1,128,1024]{2,1,0:T(8,128)(2,1)} %slice.103), channel_id=1, source_target_pairs={{0,1},{1,2},{2,3},{3,4},{4,5},{5,6},{6,7},{7,8},{8,9},{9,10},{10,1... | collective-permute-start | bytes 786440 | tf_op jit(solution)/shard_map/ppermute | solution.py:17
  250.7 6.2 copy-start.10
  250.7 12.0 %slice-start = ((s8[8388608]{0:T(1024)(128)(4,1)}), s8[4194304]{0:T(1024)(128)(4,1)S(1)}, s32[]{:S(2)}) async-start(s8[8388608]{0:T(1024)(128)(4,1)} %bitcast.171), calls=%async_computation.1 | async-start | bytes 8388608
  251.7 5.2 copy-start.12
  251.7 11.0 %slice-start.1 = ((s8[8388608]{0:T(1024)(128)(4,1)}), s8[4194304]{0:T(1024)(128)(4,1)S(1)}, s32[]{:S(2)}) async-start(s8[8388608]{0:T(1024)(128)(4,1)} %bitcast.171), calls=%async_computation.2 | async-start | bytes 8388608
  256.9 43.0 %copy-start.19 = (f32[8,1024]{1,0:T(8,128)}, f32[8,1024]{1,0:T(8,128)S(1)}, u32[]{:S(2)}) copy-start(f32[8,1024]{1,0:T(8,128)S(1)} %bitcast_maximum_fusion) | copy-start | bytes 98308
  256.9 27.5 %copy-start.21 = (f32[8,8,128]{2,1,0:T(8,128)}, f32[8,8,128]{2,1,0:T(8,128)S(1)}, u32[]{:S(2)}) copy-start(f32[8,8,128]{2,1,0:T(8,128)S(1)} %fusion.29) | copy-start | bytes 98308
  265.1 34.9 %copy-start.23 = (f32[8,1024]{1,0:T(8,128)}, f32[8,1024]{1,0:T(8,128)S(1)}, u32[]{:S(2)}) copy-start(f32[8,1024]{1,0:T(8,128)S(1)} %bitcast_add_fusion.2) | copy-start | bytes 98308
  265.1 19.3 %copy-start.25 = (f32[8,8,128]{2,1,0:T(8,128)}, f32[8,8,128]{2,1,0:T(8,128)S(1)}, u32[]{:S(2)}) copy-start(f32[8,8,128]{2,1,0:T(8,128)S(1)} %fusion.28) | copy-start | bytes 98308
  267.4 7.2 copy-start.16
  284.4 9.3 %copy-start.14 = (bf16[1,1024,1024]{1,2,0:T(8,128)(2,1)S(1)}, bf16[1,1024,1024]{1,2,0:T(8,128)(2,1)}, u32[]{:S(2)}) copy-start(bf16[1,1024,1024]{1,2,0:T(8,128)(2,1)} %copy.126) | copy-start | bytes 6291460
  284.4 15.5 %slice-start.2 = ((s8[8388608]{0:T(1024)(128)(4,1)}), s8[4194304]{0:T(1024)(128)(4,1)S(1)}, s32[]{:S(2)}) async-start(s8[8388608]{0:T(1024)(128)(4,1)} %bitcast.173), calls=%async_computation.3 | async-start | bytes 8388608
  293.8 6.2 slice-start.3
  293.8 6.2 copy-start.18
  293.8 13.4 %slice-start.6 = ((s8[8388608]{0:T(1024)(128)(4,1)}), s8[4194304]{0:T(1024)(128)(4,1)S(1)}, s32[]{:S(2)}) async-start(s8[8388608]{0:T(1024)(128)(4,1)} %bitcast.189), calls=%async_computation.7 | async-start | bytes 8388608
  300.0 7.2 slice-start.7
  307.1 17.9 %copy-start.11 = (bf16[1,8,128,8,128]{4,2,3,1,0:T(8,128)(2,1)S(1)}, bf16[1,8,128,8,128]{4,2,3,1,0:T(8,128)(2,1)}, u32[]{:S(2)}) copy-start(bf16[1,8,128,8,128]{4,2,3,1,0:T(8,128)(2,1)} %copy-done.10) | copy-start | bytes 6291460
  325.1 4.4 copy-start.1
  333.9 5.5 copy-start.20
  333.9 5.5 copy-start.24
  333.9 5.5 copy-start.26
  339.4 8.1 %copy-start.3 = (bf16[1,1024,1024]{1,2,0:T(8,128)(2,1)S(1)}, bf16[1,1024,1024]{1,2,0:T(8,128)(2,1)}, u32[]{:S(2)}) copy-start(bf16[1,1024,1024]{1,2,0:T(8,128)(2,1)} %copy.125) | copy-start | bytes 6291460
  360.4 105.3 %collective-permute-start.3 = (f32[1,128,8,128]{3,1,2,0:T(8,128)}, f32[1,128,8,128]{3,1,2,0:T(8,128)S(1)}, u32[]{:S(2)}, u32[]{:S(2)}) collective-permute-start(f32[1,128,8,128]{3,1,2,0:T(8,128)} %slice_bitcast_fusion), channel_id=1, source_target_pairs={{1,0},{2,1},{3,2},{4,3},{5,4},{6,5},{7,6},{8,7},{9,8},{10,9},{11,1... | collective-permute-start | bytes 1572872 | tf_op jit(solution)/shard_map/ppermute | solution.py:17
  361.7 9.6 %copy-start.6 = (f32[1,1024,1024]{2,1,0:T(8,128)S(1)}, f32[1,1024,1024]{2,1,0:T(8,128)}, u32[]{:S(2)}) copy-start(f32[1,1024,1024]{2,1,0:T(8,128)} %copy.94) | copy-start | bytes 12582916
  370.0 83.8 %collective-permute-start.2 = (f32[1,128,8,128]{1,3,2,0:T(8,128)}, f32[1,128,8,128]{1,3,2,0:T(8,128)S(1)}, u32[]{:S(2)}, u32[]{:S(2)}) collective-permute-start(f32[1,128,8,128]{1,3,2,0:T(8,128)} %slice_bitcast_fusion.1), channel_id=1, source_target_pairs={{1,0},{2,1},{3,2},{4,3},{5,4},{6,5},{7,6},{8,7},{9,8},{10,9},{11,1... | collective-permute-start | bytes 1572872 | tf_op jit(solution)/shard_map/ppermute | solution.py:17
  446.8 4.5 copy-start.15
  474.2 7.2 copy-start.4
  732.5 4.5 copy-start.7
  (8 other events, 23.9 us)
Sparse Core Ops, SparseCore 0:
  361.8 360.2 all-reduce.2
where the time goes:
time: 765 us; the launch traced here: 754 us
  blocking collectives  257 us (34%)
  waiting for transfers between devices  239 us (31%)
  local copies, waits for them, and re-layouts  109 us (14%)
  matrix products  78.5 us (10%)
  other arithmetic  44.2 us (6%)
  between operations  15 us (2%)
  starting transfers between devices  11.6 us (2%)
    psum x1, waiting for transfers between devices, per_device(): whole_dk, whole_dv = lax.psum((sum_dk, sum_dv), 'ctx')  239 us
    all_gather x1, blocking collectives, per_device(): lax.all_gather(own_sum_values, 'ctx', axis=1, tiled=True)  95.3 us
    all_gather x1, blocking collectives, per_device(): lax.all_gather(own_sum_keys, 'ctx', axis=1, tiled=True)  93.4 us
    psum x1, blocking collectives, per_device(): gain_total = lax.psum(gain_part, ('dp', 'ctx'))  68.5 us
    unnamed x83, local copies, waits for them, and re-layouts  36.2 us
    dot_general x1, matrix products, per_device(): jnp.einsum('bnqhd,bnkhd->bnhqk', grad_blocks, band_values, preferred_elem...  17.9 us
  transfers between devices with their start and end apart: 5, of which 1 were waited for; matrix products, arithmetic and copies ran while one was open for 14% of the time, Pallas kernels for 0%

commit v1 on v0

--- a/solution.py
+++ b/solution.py
@@ -9,6 +9,11 @@
 STRIDE = 1024
 SUMMARY = 8
 NEG = -1e30
+
+
+def swapped_in(x, name, dim):
+    sent = jnp.stack([x] * lax.axis_size(name))
+    return jnp.concatenate(lax.all_to_all(sent, name, 0, 0), axis=dim)
 
 
 def from_behind(value, axis, steps):
@@ -48,7 +53,7 @@
         batch, own_sums, width
     )
     sum_keys, sum_values = (
-        lax.all_gather(own_sum_keys, "ctx", axis=1, tiled=True),
+        swapped_in(own_sum_keys, "ctx", 1),
         lax.all_gather(own_sum_values, "ctx", axis=1, tiled=True),
     )
     total_sums = sum_keys.shape[1]

time: 765 us -> 682 us (0.89)
  blocking collectives: 257 us -> 171 us
  starting transfers between devices: 11.6 us -> 20.5 us
    all_gather x1 -> x0, blocking collectives: 93.4 us -> none  [per_device(): lax.all_gather(own_sum_keys, 'ctx', axis=1, tiled=True)]
    all_to_all x0 -> x1, starting transfers between devices: none -> 8.89 us  [swapped_in(): return jnp.concatenate(lax.all_to_all(sent, name, 0, 0), axis=dim)]
    unnamed x83 -> x82, local copies, waits for them, and re-layouts: 36.2 us -> 37.5 us
  transfers between devices with their start and end apart: 5 -> 6, of which waited for: 1 -> 1; matrix products, arithmetic and copies ran while one was open for 14% -> 15% of each run, Pallas kernels for 0% -> 0%
where the time goes in v1:
time: 682 us; the launch traced here: 671 us
  waiting for transfers between devices  235 us (34%)
  blocking collectives  171 us (25%)
  local copies, waits for them, and re-layouts  113 us (17%)
  matrix products  75 us (11%)
  other arithmetic  41.7 us (6%)
  starting transfers between devices  20.5 us (3%)
  between operations  15.1 us (2%)
    psum x1, waiting for transfers between devices, per_device(): whole_dk, whole_dv = lax.psum((sum_dk, sum_dv), 'ctx')  235 us
    all_gather x1, blocking collectives, per_device(): lax.all_gather(own_sum_values, 'ctx', axis=1, tiled=True)  102 us
    psum x1, blocking collectives, per_device(): gain_total = lax.psum(gain_part, ('dp', 'ctx'))  68.7 us
    unnamed x82, local copies, waits for them, and re-layouts  37.5 us
    dot_general x1, matrix products, per_device(): jnp.einsum('bnqhd,bnkhd->bnhqk', grad_blocks, band_values, preferred_elem...  17.4 us
  transfers between devices with their start and end apart: 6, of which 1 were waited for; matrix products, arithmetic and copies ran while one was open for 15% of the time, Pallas kernels for 0%

profile of v1, /device:TPU:8, one launch (start us, length us, event | category | flops | bytes accessed | tf_op | source)
XLA Modules:
  0.0 671.3 jit_solution(14463277451742916610)
XLA Ops:
  9.0 4.2 collective-permute-start
  14.9 4.8 collective-permute-start.1
  21.3 8.9 %all-to-all-start = ((bf16[32,1,8,1024]{3,2,1,0:T(8,128)(2,1)}), bf16[32,1,8,1024]{3,2,1,0:T(8,128)(2,1)S(1)}, u32[]{:S(2)}, u32[]{:S(2)}) async-start(bf16[32,1,8,1024]{3,2,1,0:T(8,128)(2,1)} %stack.3), calls=%async_computation | async-start | bytes 1048576 | tf_op jit(solution)/shard_map/all_to_all | solution.py:16
  36.5 102.5 %all-gather = bf16[1,1,256,1024]{3,2,1,0:T(8,128)(2,1)} all-gather(bf16[1,1,8,1024]{3,2,1,0:T(8,128)(2,1)S(1)} %slice.124), channel_id=2, replica_groups=mesh['dp'=4,'ctx'=32] {'ctx'}, dimensions={2}, use_global_device_ids=true | all-gather | bytes 540672 | tf_op jit(solution)/shard_map/all_gather | solution.py:57
  143.3 4.1 copy.85
  155.2 4.1 copy.95
  174.3 5.1 fusion.2
  195.4 4.3 copy.80
  199.7 5.4 copy.83
  205.2 9.3 %convolution_bitcast_fusion = f32[1,8,256,8,128]{4,2,3,1,0:T(8,128)} fusion(bf16[8,128,8,128]{3,2,1,0:T(8,128)(2,1)} %bitcast.199, f32[8,8,128,256]{3,2,1,0:T(8,128)} %get-tuple-element.53, f32[8,8,128]{2,1,0:T(8,128)S(1)} %fusion.28, f32[8,8,128]{2,1,0:T(8,128)S(1)} %fusion.29, pred[8,128,256]{2,1,0:T(8,128)(4,1)S(1)} %broadcast_and_fusion), kind=kOutput, calls=%fused_computation.27 | convolution fusion | flops 549453824 | bytes 19202048 | tf_op jit(solution)/shard_map/bnhqk,bnqhd->bnkhd/dot_general | solution.py:113
  214.5 6.2 fusion.16
  220.7 7.3 %multiply_reduce_fusion = (f32[1024,8]{0,1:T(8,128)}, bf16[1,1024,8,128]{1,3,2,0:T(8,128)(2,1)}) fusion(f32[1,1024,8,128]{1,3,2,0:T(8,128)} %bitcast.194, f32[1,1024,8,128]{1,3,2,0:T(8,128)} %copy.83, bf16[256,8,128]{0,2,1:T(8,128)(2,1)S(1)} %bitcast.208, f32[8,1024]{1,0:T(8,128)S(1)} %bitcast_add_fusion.2, f32[8,1024]{1,0:T(8,128)S(1)} %bitcast_maximum_fusion, ...), kind=kOutput, calls=%fused_computation.26 | convolution fusion | flops 554688512 | bytes 19759104 | tf_op jit(solution)/shard_map/bhqs,bshd->bqhd/dot_general | solution.py:100
  228.0 17.4 %fusion.1 = bf16[8,8,128,256]{3,2,1,0:T(8,128)(2,1)S(1)} fusion(f32[8,8,128]{2,1,0:T(8,128)} %bitcast.209, bf16[1,8,128,8,128]{4,2,3,1,0:T(8,128)(2,1)} %copy.123, bf16[1,8,128,8,128]{4,2,3,1,0:T(8,128)(2,1)} %copy.122, bf16[8,128,8,128]{3,2,1,0:T(8,128)(2,1)} %bitcast.200, f32[8,8,128]{2,1,0:T(8,128)} %copy-done.28, f32[8,8,128]{2,1,0:T(8,128)} %copy-done.23, ...), kind=kOutput, calls=%fused_computation.2 | convolution fusion | flops 564133888 | bytes 19234816 | tf_op jit(solution)/shard_map/bnqhd,bnkhd->bnhqk/dot_general | solution.py:107
  245.4 4.4 fusion.14
  249.9 4.4 copy.87
  254.3 5.4 copy.93
  259.7 8.1 %multiply_convert_fusion = bf16[8,1024,256]{1,2,0:T(8,128)(2,1)S(1)} fusion(f32[8,1024]{1,0:T(8,128)S(1)} %bitcast.210, bf16[1024,8,128]{0,2,1:T(8,128)(2,1)} %bitcast.197, bf16[256,8,128]{0,2,1:T(8,128)(2,1)} %bitcast.207, f32[8,1024]{1,0:T(8,128)S(1)} %copy-done.27, f32[8,1024]{1,0:T(8,128)S(1)} %copy-done.22, f32[8,1024,256]{1,2,0:T(8,128)} %copy-done.1, ...), kind=kOutput, calls=%fused_computation.3 | convolution fusion | flops 555745280 | bytes 15564800 | tf_op jit(solution)/shard_map/bqhd,bshd->bhqs/dot_general | solution.py:110
  273.3 5.4 copy.94
  282.0 4.2 convolution_bitcast_fusion.1
  293.7 68.7 %psum.23 = f32[1024]{0:T(1024)S(1)} all-reduce(f32[1024]{0:T(1024)S(1)} %get-tuple-element.46), channel_id=1, replica_groups=mesh['dp'=4,'ctx'=32] {'dp','ctx'}, use_global_device_ids=true, to_apply=%region_8.9 | all-reduce | flops 1024 | bytes 8192 | tf_op jit(solution)/shard_map/psum | solution.py:143
  362.9 4.3 slice.126
  367.3 4.4 slice.130
  374.2 6.3 slice_add_fusion.1
  380.6 5.6 copy.96
  386.2 4.1 slice_add_fusion
  390.3 4.4 copy.103
  394.7 7.2 %copy.138 = f32[1,1024,1024]{2,0,1:T(1,128)} copy(f32[1,1024,1024]{2,0,1:T(1,128)} %bitcast.185) | data formatting | bytes 8388608
  403.8 235.2 %all-reduce.3.cloned.1.call-done = (f32[1,256,1024]{1,2,0:T(8,128)}, f32[1,256,1024]{1,2,0:T(8,128)}) async-done(((f32[1,256,1024]{1,2,0:T(8,128)}, f32[1,256,1024]{1,2,0:T(8,128)}), (f32[1,256,1024]{1,2,0:T(8,128)}, f32[1,256,1024]{1,2,0:T(8,128)})) %all-reduce.3.cloned.1.call-update) | async-done | bytes 2097168 | tf_op jit(solution)/shard_map/psum | solution.py:122
  642.3 7.1 %convert_element_type.88 = bf16[1,1024,1024]{2,0,1:T(2,128)(2,1)} convert(f32[1,1024,1024]{2,0,1:T(1,128)} %fusion.25) | non-fusion elementwise | flops 1048576 | bytes 6291456 | tf_op jit(solution)/shard_map/convert_element_type | solution.py:130
  649.3 4.5 copy.111
  654.6 5.1 convert_element_type.87
  659.7 4.3 copy.110
  (133 shorter events, 79.5 us)
Async XLA Ops:
  7.2 26.6 %copy-start.25 = (f32[1024]{0:T(1024)S(1)}, f32[1024]{0:T(1024)}, u32[]{:S(2)}) copy-start(f32[1024]{0:T(1024)} %param.13) | copy-start | bytes 12292
  7.2 26.6 %copy-start.3 = (bf16[1,1024,1024]{2,1,0:T(8,128)(2,1)S(1)}, bf16[1,1024,1024]{2,1,0:T(8,128)(2,1)}, u32[]{:S(2)}) copy-start(bf16[1,1024,1024]{2,1,0:T(8,128)(2,1)} %param.9) | copy-start | bytes 6291460
  9.0 159.1 %collective-permute-start = (bf16[1,128,1024]{2,1,0:T(8,128)(2,1)}, bf16[1,128,1024]{2,1,0:T(8,128)(2,1)S(1)}, u32[]{:S(2)}, u32[]{:S(2)}) collective-permute-start(bf16[1,128,1024]{2,1,0:T(8,128)(2,1)} %slice.102), channel_id=1, source_target_pairs={{0,1},{1,2},{2,3},{3,4},{4,5},{5,6},{6,7},{7,8},{8,9},{9,10},{10,1... | collective-permute-start | bytes 786440 | tf_op jit(solution)/shard_map/ppermute | solution.py:22
  14.9 148.4 %collective-permute-start.1 = (bf16[1,128,1024]{2,1,0:T(8,128)(2,1)}, bf16[1,128,1024]{2,1,0:T(8,128)(2,1)}, u32[]{:S(2)}, u32[]{:S(2)}) collective-permute-start(bf16[1,128,1024]{2,1,0:T(8,128)(2,1)} %slice.105), channel_id=1, source_target_pairs={{0,1},{1,2},{2,3},{3,4},{4,5},{5,6},{6,7},{7,8},{8,9},{9,10},{10,1... | collective-permute-start | bytes 786440 | tf_op jit(solution)/shard_map/ppermute | solution.py:22
  21.3 158.2 %all-to-all-start = ((bf16[32,1,8,1024]{3,2,1,0:T(8,128)(2,1)}), bf16[32,1,8,1024]{3,2,1,0:T(8,128)(2,1)S(1)}, u32[]{:S(2)}, u32[]{:S(2)}) async-start(bf16[32,1,8,1024]{3,2,1,0:T(8,128)(2,1)} %stack.3), calls=%async_computation | async-start | bytes 1048576 | tf_op jit(solution)/shard_map/all_to_all | solution.py:16
  30.2 608.8 %all-reduce.3.cloned.1.call-start = ((), (), s32[]{:S(2)}) async-start(), calls=%async_computation.1 | async-start | bytes 4194304 | tf_op jit(solution)/shard_map/psum | solution.py:122
  167.5 6.8 %copy-start.12 = (bf16[1,8,128,8,128]{4,2,3,1,0:T(8,128)(2,1)}, bf16[1,8,128,8,128]{4,2,3,1,0:T(8,128)(2,1)S(1)}, u32[]{:S(2)}) copy-start(bf16[1,8,128,8,128]{4,2,3,1,0:T(8,128)(2,1)S(1)} %copy.120) | copy-start | bytes 6291460
  168.1 6.2 copy-start.14
  170.5 3.8 copy-start.9
  181.7 4.0 copy-start.11
  185.2 35.4 %copy-start.21 = (f32[8,1024]{1,0:T(8,128)}, f32[8,1024]{1,0:T(8,128)S(1)}, u32[]{:S(2)}) copy-start(f32[8,1024]{1,0:T(8,128)S(1)} %bitcast_maximum_fusion) | copy-start | bytes 98308
  185.3 19.9 %copy-start.23 = (f32[8,8,128]{2,1,0:T(8,128)}, f32[8,8,128]{2,1,0:T(8,128)S(1)}, u32[]{:S(2)}) copy-start(f32[8,8,128]{2,1,0:T(8,128)S(1)} %fusion.29) | copy-start | bytes 98308
  191.3 29.4 %copy-start.26 = (f32[8,1024]{1,0:T(8,128)}, f32[8,1024]{1,0:T(8,128)S(1)}, u32[]{:S(2)}) copy-start(f32[8,1024]{1,0:T(8,128)S(1)} %bitcast_add_fusion.2) | copy-start | bytes 98308
  191.3 13.8 %copy-start.28 = (f32[8,8,128]{2,1,0:T(8,128)}, f32[8,8,128]{2,1,0:T(8,128)S(1)}, u32[]{:S(2)}) copy-start(f32[8,8,128]{2,1,0:T(8,128)S(1)} %fusion.28) | copy-start | bytes 98308
  205.1 9.3 %copy-start.16 = (bf16[1,1024,1024]{1,2,0:T(8,128)(2,1)S(1)}, bf16[1,1024,1024]{1,2,0:T(8,128)(2,1)}, u32[]{:S(2)}) copy-start(bf16[1,1024,1024]{1,2,0:T(8,128)(2,1)} %copy.125) | copy-start | bytes 6291460
  205.1 15.5 %slice-start = ((s8[8388608]{0:T(1024)(128)(4,1)}), s8[4194304]{0:T(1024)(128)(4,1)S(1)}, s32[]{:S(2)}) async-start(s8[8388608]{0:T(1024)(128)(4,1)} %bitcast.176), calls=%async_computation.2 | async-start | bytes 8388608
  214.5 6.2 slice-start.1
  214.5 6.2 copy-start.20
  214.5 13.5 %slice-start.2 = ((s8[8388608]{0:T(1024)(128)(4,1)}), s8[4194304]{0:T(1024)(128)(4,1)S(1)}, s32[]{:S(2)}) async-start(s8[8388608]{0:T(1024)(128)(4,1)} %bitcast.190), calls=%async_computation.4 | async-start | bytes 8388608
  220.7 7.3 %slice-start.3 = ((s8[8388608]{0:T(1024)(128)(4,1)}), s8[4194304]{0:T(1024)(128)(4,1)S(1)}, s32[]{:S(2)}) async-start(s8[8388608]{0:T(1024)(128)(4,1)} %bitcast.190), calls=%async_computation.5 | async-start | bytes 8388608
  228.0 17.4 %copy-start.13 = (bf16[1,8,128,8,128]{4,2,3,1,0:T(8,128)(2,1)S(1)}, bf16[1,8,128,8,128]{4,2,3,1,0:T(8,128)(2,1)}, u32[]{:S(2)}) copy-start(bf16[1,8,128,8,128]{4,2,3,1,0:T(8,128)(2,1)} %copy-done.12) | copy-start | bytes 6291460
  245.4 4.4 copy-start.2
  254.3 5.4 copy-start.22
  254.3 5.4 copy-start.27
  254.3 5.4 copy-start.29
  259.7 8.1 %copy-start.4 = (bf16[1,1024,1024]{1,2,0:T(8,128)(2,1)S(1)}, bf16[1,1024,1024]{1,2,0:T(8,128)(2,1)}, u32[]{:S(2)}) copy-start(bf16[1,1024,1024]{1,2,0:T(8,128)(2,1)} %copy.124) | copy-start | bytes 6291460
  280.6 105.5 %collective-permute-start.3 = (f32[1,128,8,128]{3,1,2,0:T(8,128)}, f32[1,128,8,128]{3,1,2,0:T(8,128)S(1)}, u32[]{:S(2)}, u32[]{:S(2)}) collective-permute-start(f32[1,128,8,128]{3,1,2,0:T(8,128)} %slice_bitcast_fusion), channel_id=1, source_target_pairs={{1,0},{2,1},{3,2},{4,3},{5,4},{6,5},{7,6},{8,7},{9,8},{10,9},{11,1... | collective-permute-start | bytes 1572872 | tf_op jit(solution)/shard_map/ppermute | solution.py:22
  281.9 9.6 %copy-start.7 = (f32[1,1024,1024]{2,1,0:T(8,128)S(1)}, f32[1,1024,1024]{2,1,0:T(8,128)}, u32[]{:S(2)}) copy-start(f32[1,1024,1024]{2,1,0:T(8,128)} %copy.94) | copy-start | bytes 12582916
  290.2 84.0 %collective-permute-start.2 = (f32[1,128,8,128]{1,3,2,0:T(8,128)}, f32[1,128,8,128]{1,3,2,0:T(8,128)S(1)}, u32[]{:S(2)}, u32[]{:S(2)}) collective-permute-start(f32[1,128,8,128]{1,3,2,0:T(8,128)} %slice_bitcast_fusion.1), channel_id=1, source_target_pairs={{1,0},{2,1},{3,2},{4,3},{5,4},{6,5},{7,6},{8,7},{9,8},{10,9},{11,1... | collective-permute-start | bytes 1572872 | tf_op jit(solution)/shard_map/ppermute | solution.py:22
  367.3 4.4 copy-start.17
  394.7 7.2 %copy-start.5 = (f32[1,8,128,8,128]{4,3,0,2,1:T(8,128)S(1)}, f32[1,8,128,8,128]{4,3,0,2,1:T(8,128)}, u32[]{:S(2)}) copy-start(f32[1,8,128,8,128]{4,3,0,2,1:T(8,128)} %copy.96) | copy-start | bytes 12582916
  649.3 4.5 copy-start.8
  (8 other events, 23.1 us)
Sparse Core Ops, SparseCore 0:
  282.1 356.8 all-reduce.2
